TPU v7x, 32 devices: a whole 2x2x4 slice. The times are simulated.
32 devices in a mesh: docs: 8 (over z, x), heads: 4 (over y, core).
Axes of the slice: x: 2, y: 2, z: 4, core: 2. Of those that a mesh axis runs over, the one named last changes fastest.
Arguments:
- tokens: bfloat16 [10240, 768], P('docs'), may hold values from -6 to 6
- seg_index: int32 [16, 512], P('docs'), may hold values from 0 to 127, as said below
- seg_count: int32 [16], P('docs'), may hold values from 5 to 128, as said below
- weight_query: float32 [768, 768], P('docs', 'heads'), may hold values from -0.21875 to 0.21875
- weight_key: float32 [768, 768], P('docs', 'heads'), may hold values from -0.21875 to 0.21875
- weight_value: float32 [768, 768], P('docs', 'heads'), may hold values from -0.21875 to 0.21875
- weight_out: float32 [768, 768], P('heads', 'docs'), may hold values from -3.5 to 3.5
- weight_up: float32 [768, 3072], P('docs', 'heads'), may hold values from -0.21875 to 0.21875
- weight_down: float32 [3072, 768], P('heads', 'docs'), may hold values from -0.109375 to 0.109375
- bias_query: float32 [768], P('heads'), may hold values from -3 to 3
- bias_value: float32 [768], P('heads'), may hold values from -3 to 3
- bias_out: float32 [768], replicated, may hold values from -2 to 2
- bias_up: float32 [3072], P('heads'), may hold values from -2 to 2
- bias_down: float32 [768], replicated, may hold values from -2 to 2
- gain_one: float32 [768], replicated, may hold values from 0.25 to 1.75
- shift_one: float32 [768], replicated, may hold values from -2 to 2
- gain_two: float32 [768], replicated, may hold values from 0.25 to 1.75
- shift_two: float32 [768], replicated, may hold values from -2 to 2
- cotangent: bfloat16 [10240, 768], P('docs'), may hold values from -6 to 6
Outputs:
- layer_out: bfloat16 [10240, 768], P(('docs', 'heads'))
- grad_tokens: bfloat16 [10240, 768], P('docs')
- gradient_weight_query: float32 [768, 768], P('docs', 'heads')
- gradient_weight_key: float32 [768, 768], P('docs', 'heads')
- gradient_weight_value: float32 [768, 768], P('docs', 'heads')
- gradient_weight_out: float32 [768, 768], P('heads', 'docs')
- gradient_weight_up: float32 [768, 3072], P('docs', 'heads')
- gradient_weight_down: float32 [3072, 768], P('heads', 'docs')
- gradient_bias_query: float32 [768], P('heads')
- gradient_bias_value: float32 [768], P('heads')
- gradient_bias_out: float32 [768], replicated
- gradient_bias_up: float32 [3072], P('heads')
- gradient_bias_down: float32 [768], replicated
- gradient_gain_one: float32 [768], replicated
- gradient_shift_one: float32 [768], replicated
- gradient_gain_two: float32 [768], replicated
- gradient_shift_two: float32 [768], replicated
Inputs may be any that keep to these rules, and one draw needn't show every extreme that they name: `seg_count`: one document of each draw has exactly 128 segments. seg_index[d, t] is below seg_count[d]; the first text token of each document belongs to its last segment.
All inputs are finite; a program needn't handle non-finite values.
Results may differ from a plain program's by a relative error of at most 0.02.
Values may be sent and summed in bfloat16 or wider, within the bound.
No kernel may reach another device: no remote copies, remote signals or barrier semaphores. Data moves between devices by JAX's collectives and lax.ppermute only.
A program may use at most 128 MiB of HBM per device.

v0:
```python
from functools import partial

import jax
import jax.numpy as jnp
from jax import lax
from jax.sharding import PartitionSpec as P

HEAD_DIM = 64


epsilon = 1e-05
masked_score = -1000000000.0


def norm_forward(pre_rows, gain_vec, shift_vec):
    average = jnp.mean(pre_rows, axis=-1, keepdims=True)
    centered = pre_rows - average
    variance = jnp.mean(centered * centered, axis=-1, keepdims=True)
    inv_std = lax.rsqrt(variance + epsilon)
    scaled = centered * inv_std
    return (scaled * gain_vec + shift_vec, scaled, inv_std)


def norm_backward(grad_out, scaled, inv_std, gain_vec):
    grad_scaled = grad_out * gain_vec
    mean_grad = jnp.mean(grad_scaled, axis=-1, keepdims=True)
    mean_along = jnp.mean(grad_scaled * scaled, axis=-1, keepdims=True)
    return inv_std * (grad_scaled - mean_grad - scaled * mean_along)


def contract_rows(left_side, right_side):
    return lax.dot_general(
        left_side, right_side, (((0,), (0,)), ((), ())), preferred_element_type=jnp.float32
    )


def contract_cols(left_side, right_side):
    return lax.dot_general(
        left_side, right_side, (((1,), (1,)), ((), ())), preferred_element_type=jnp.float32
    )


def score_block(queries, key_rows, seg_total, text_len):
    score_scale = queries.shape[-1] ** (-0.5)
    scores = (
        jnp.einsum("qhd,khd->hqk", queries, key_rows, preferred_element_type=jnp.float32)
        * score_scale
    )
    visible = jnp.arange(key_rows.shape[0], dtype=jnp.int32) < text_len + seg_total
    return jnp.where(visible[None, None, :], scores, masked_score)


def attend_forward(text_len, pieces):
    queries, key_rows, value_rows, seg_total = pieces
    scores = score_block(queries, key_rows, seg_total, text_len)
    top_score = jnp.max(scores, axis=-1, keepdims=True)
    raised = jnp.exp(scores - top_score)
    totals = jnp.sum(raised, axis=-1, keepdims=True)
    probs_low = (raised / totals).astype(jnp.bfloat16)
    context = jnp.einsum("hqk,khd->qhd", probs_low, value_rows, preferred_element_type=jnp.float32)
    return (context.astype(jnp.bfloat16), (top_score + jnp.log(totals))[..., 0])


def attend_backward(text_len, pieces):
    queries, key_rows, value_rows, seg_total, log_total, grad_context = pieces
    scores = score_block(queries, key_rows, seg_total, text_len)
    attn_probs = jnp.exp(scores - log_total[..., None])
    grad_probs = jnp.einsum(
        "qhd,khd->hqk", grad_context, value_rows, preferred_element_type=jnp.float32
    )
    inner_sum = jnp.sum(grad_probs * attn_probs, axis=-1, keepdims=True)
    grad_scores = (attn_probs * (grad_probs - inner_sum)).astype(jnp.bfloat16)
    score_scale = queries.shape[-1] ** (-0.5)
    grad_values = jnp.einsum(
        "hqk,qhd->khd",
        attn_probs.astype(jnp.bfloat16),
        grad_context,
        preferred_element_type=jnp.float32,
    )
    grad_queries = (
        jnp.einsum("hqk,khd->qhd", grad_scores, key_rows, preferred_element_type=jnp.float32)
        * score_scale
    )
    grad_keys = (
        jnp.einsum("hqk,qhd->khd", grad_scores, queries, preferred_element_type=jnp.float32)
        * score_scale
    )
    return (
        grad_queries.astype(jnp.bfloat16),
        grad_keys.astype(jnp.bfloat16),
        grad_values.astype(jnp.bfloat16),
    )


def body(
    tokens,
    seg_index,
    seg_count,
    weight_query,
    weight_key,
    weight_value,
    weight_out,
    weight_up,
    weight_down,
    bias_query,
    bias_value,
    bias_out,
    bias_up,
    bias_down,
    gain_one,
    shift_one,
    gain_two,
    shift_two,
    cotangent,
):
    docs_here = seg_count.shape[0]
    model_width = tokens.shape[1]
    row_count = tokens.shape[0]
    seq_len = row_count // docs_here
    text_len = seg_index.shape[1]
    slot_total = seq_len - text_len
    head_size = HEAD_DIM
    heads_here = weight_query.shape[1] // head_size
    heads_pos = lax.axis_index("heads")
    share_rows = row_count // lax.axis_size("heads")
    row_start = heads_pos * share_rows

    def local_rows(array):
        return lax.dynamic_slice_in_dim(array, row_start, share_rows, 0)

    full_query, full_key, full_value, full_out, full_up, full_down = (
        lax.all_gather(weight_query.astype(jnp.bfloat16), "docs", axis=0, tiled=True),
        lax.all_gather(weight_key.astype(jnp.bfloat16), "docs", axis=0, tiled=True),
        lax.all_gather(weight_value.astype(jnp.bfloat16), "docs", axis=0, tiled=True),
        lax.all_gather(weight_out.astype(jnp.bfloat16), "docs", axis=1, tiled=True),
        lax.all_gather(weight_up.astype(jnp.bfloat16), "docs", axis=0, tiled=True),
        lax.all_gather(weight_down.astype(jnp.bfloat16), "docs", axis=1, tiled=True),
    )
    shaped = tokens.reshape(docs_here, seq_len, model_width)
    text_rows = shaped[:, :text_len]
    slot_ids = jnp.arange(slot_total, dtype=jnp.int32)
    onehot = (seg_index[:, :, None] == slot_ids[None, None, :]).astype(jnp.bfloat16)
    members = jnp.sum(onehot.astype(jnp.float32), axis=1)
    divisor = jnp.maximum(members, 1.0)[:, :, None]
    pooled = (
        jnp.einsum("gts,gtd->gsd", onehot, text_rows, preferred_element_type=jnp.float32) / divisor
    )
    slot_live = (slot_ids[None, :] < seg_count[:, None]).astype(jnp.float32)
    slot_rows = slot_live[:, :, None] * (shaped[:, text_len:].astype(jnp.float32) + pooled)
    inputs = jnp.concatenate([text_rows.astype(jnp.float32), slot_rows], axis=1).reshape(
        row_count, model_width
    )
    hidden_in = inputs.astype(jnp.bfloat16)
    queries = (
        jnp.dot(hidden_in, full_query, preferred_element_type=jnp.float32) + bias_query
    ).astype(jnp.bfloat16)
    key_rows = jnp.dot(hidden_in, full_key, preferred_element_type=jnp.float32).astype(jnp.bfloat16)
    value_rows = (
        jnp.dot(hidden_in, full_value, preferred_element_type=jnp.float32) + bias_value
    ).astype(jnp.bfloat16)
    head_shape = (docs_here, seq_len, heads_here, head_size)
    query_heads = queries.reshape(head_shape)
    key_heads = key_rows.reshape(head_shape)
    value_heads = value_rows.reshape(head_shape)
    context, log_total = lax.map(
        partial(attend_forward, text_len), (query_heads, key_heads, value_heads, seg_count)
    )
    context_flat = context.reshape(row_count, heads_here * head_size)
    attn_part = jnp.dot(context_flat, full_out, preferred_element_type=jnp.float32)
    attn_total = lax.psum(attn_part, "heads")
    pre_one = inputs + (attn_total + bias_out)
    normed_one, scaled_one, inv_one = norm_forward(pre_one, gain_one, shift_one)
    normed_low = normed_one.astype(jnp.bfloat16)
    upward = jnp.dot(normed_low, full_up, preferred_element_type=jnp.float32) + bias_up
    activated = jax.nn.gelu(upward, approximate=False).astype(jnp.bfloat16)
    down_part = jnp.dot(activated, full_down, preferred_element_type=jnp.float32)
    down_total = lax.psum(down_part.astype(jnp.bfloat16), "heads").astype(jnp.float32)
    grad_rows_out = cotangent.astype(jnp.float32)
    pre_two = normed_one + (down_total + bias_down)
    normed_two, scaled_two, inv_two = norm_forward(pre_two, gain_two, shift_two)
    layer_out = local_rows(normed_two).astype(jnp.bfloat16)
    grad_pre_two = norm_backward(grad_rows_out, scaled_two, inv_two, gain_two)
    gain_two_part = jnp.sum(local_rows(grad_rows_out * scaled_two), axis=0)
    shift_two_part = jnp.sum(local_rows(grad_rows_out), axis=0)
    grad_down_low = grad_pre_two.astype(jnp.bfloat16)
    bias_down_part = jnp.sum(local_rows(grad_down_low.astype(jnp.float32)), axis=0)
    grad_weight_down = contract_rows(activated, grad_down_low)
    grad_activated = contract_cols(grad_down_low, full_down)
    gelu_value, gelu_back = jax.vjp(partial(jax.nn.gelu, approximate=False), upward)
    grad_up_low = gelu_back(grad_activated)[0].astype(jnp.bfloat16)
    grad_weight_up = contract_rows(normed_low, grad_up_low)
    bias_up_part = jnp.sum(grad_up_low.astype(jnp.float32), axis=0)
    grad_normed_part = contract_cols(grad_up_low, full_up)
    grad_normed = (
        lax.psum(grad_normed_part.astype(jnp.bfloat16), "heads").astype(jnp.float32) + grad_pre_two
    )
    grad_pre_one = norm_backward(grad_normed, scaled_one, inv_one, gain_one)
    gain_one_part = jnp.sum(local_rows(grad_normed * scaled_one), axis=0)
    shift_one_part = jnp.sum(local_rows(grad_normed), axis=0)
    grad_branch_low = grad_pre_one.astype(jnp.bfloat16)
    bias_out_part = jnp.sum(local_rows(grad_branch_low.astype(jnp.float32)), axis=0)
    grad_weight_out = contract_rows(context_flat, grad_branch_low)
    grad_context = contract_cols(grad_branch_low, full_out).astype(jnp.bfloat16)
    grad_query_heads, grad_key_heads, grad_value_heads = lax.map(
        partial(attend_backward, text_len),
        (
            query_heads,
            key_heads,
            value_heads,
            seg_count,
            log_total,
            grad_context.reshape(head_shape),
        ),
    )
    local_width = heads_here * head_size
    grad_queries = grad_query_heads.reshape(row_count, local_width)
    grad_keys = grad_key_heads.reshape(row_count, local_width)
    grad_values = grad_value_heads.reshape(row_count, local_width)
    grad_weight_query = contract_rows(hidden_in, grad_queries)
    grad_weight_key = contract_rows(hidden_in, grad_keys)
    grad_weight_value = contract_rows(hidden_in, grad_values)
    bias_query_part = jnp.sum(grad_queries.astype(jnp.float32), axis=0)
    bias_value_part = jnp.sum(grad_values.astype(jnp.float32), axis=0)
    grad_hidden_part = (
        contract_cols(grad_queries, full_query)
        + contract_cols(grad_keys, full_key)
        + contract_cols(grad_values, full_value)
    )
    grad_summed = (
        lax.psum(grad_hidden_part.astype(jnp.bfloat16), "heads").astype(jnp.float32) + grad_pre_one
    )
    grad_inputs = lax.optimization_barrier(grad_summed.astype(jnp.bfloat16)).astype(jnp.float32)
    grad_shaped = grad_inputs.reshape(docs_here, seq_len, model_width)
    grad_slots = slot_live[:, :, None] * grad_shaped[:, text_len:]
    spread_back = jnp.einsum(
        "gts,gsd->gtd",
        onehot.astype(jnp.float32),
        grad_slots / divisor,
        precision=lax.Precision.HIGHEST,
        preferred_element_type=jnp.float32,
    )
    grad_text = grad_shaped[:, :text_len] + spread_back
    grad_tokens = (
        jnp.concatenate([grad_text, grad_slots], axis=1)
        .reshape(row_count, model_width)
        .astype(jnp.bfloat16)
    )
    (
        gradient_weight_query,
        gradient_weight_key,
        gradient_weight_value,
        gradient_weight_out,
        gradient_weight_up,
        gradient_weight_down,
    ) = (
        lax.psum_scatter(
            grad_weight_query.astype(jnp.bfloat16), "docs", scatter_dimension=0, tiled=True
        ).astype(jnp.float32),
        lax.psum_scatter(
            grad_weight_key.astype(jnp.bfloat16), "docs", scatter_dimension=0, tiled=True
        ).astype(jnp.float32),
        lax.psum_scatter(
            grad_weight_value.astype(jnp.bfloat16), "docs", scatter_dimension=0, tiled=True
        ).astype(jnp.float32),
        lax.psum_scatter(
            grad_weight_out.astype(jnp.bfloat16), "docs", scatter_dimension=1, tiled=True
        ).astype(jnp.float32),
        lax.psum_scatter(
            grad_weight_up.astype(jnp.bfloat16), "docs", scatter_dimension=0, tiled=True
        ).astype(jnp.float32),
        lax.psum_scatter(
            grad_weight_down.astype(jnp.bfloat16), "docs", scatter_dimension=1, tiled=True
        ).astype(jnp.float32),
    )

    def widen(part_vec):
        wide_vec = jnp.zeros((part_vec.shape[0] * lax.axis_size("heads"),), jnp.float32)
        return lax.dynamic_update_slice_in_dim(wide_vec, part_vec, heads_pos * part_vec.shape[0], 0)

    (
        wide_query,
        wide_value,
        wide_up,
        gradient_bias_out,
        gradient_bias_down,
        gradient_gain_one,
        gradient_shift_one,
        gradient_gain_two,
        gradient_shift_two,
    ) = lax.psum(
        (
            widen(bias_query_part),
            widen(bias_value_part),
            widen(bias_up_part),
            bias_out_part,
            bias_down_part,
            gain_one_part,
            shift_one_part,
            gain_two_part,
            shift_two_part,
        ),
        ("docs", "heads"),
    )
    gradient_bias_query = lax.dynamic_slice_in_dim(
        wide_query, heads_pos * bias_query_part.shape[0], bias_query_part.shape[0], 0
    )
    gradient_bias_value = lax.dynamic_slice_in_dim(
        wide_value, heads_pos * bias_value_part.shape[0], bias_value_part.shape[0], 0
    )
    gradient_bias_up = lax.dynamic_slice_in_dim(
        wide_up, heads_pos * bias_up_part.shape[0], bias_up_part.shape[0], 0
    )
    return (
        layer_out,
        grad_tokens,
        gradient_weight_query,
        gradient_weight_key,
        gradient_weight_value,
        gradient_weight_out,
        gradient_weight_up,
        gradient_weight_down,
        gradient_bias_query,
        gradient_bias_value,
        gradient_bias_out,
        gradient_bias_up,
        gradient_bias_down,
        gradient_gain_one,
        gradient_shift_one,
        gradient_gain_two,
        gradient_shift_two,
    )


def solution(mesh):
    placed = (
        P("docs", None),
        P("docs", None),
        P("docs"),
        P("docs", "heads"),
        P("docs", "heads"),
        P("docs", "heads"),
        P("heads", "docs"),
        P("docs", "heads"),
        P("heads", "docs"),
        P("heads"),
        P("heads"),
        P(),
        P("heads"),
        P(),
        P(),
        P(),
        P(),
        P(),
        P("docs", None),
    )
    return jax.shard_map(
        body,
        mesh=mesh,
        in_specs=placed,
        out_specs=(
            P(("docs", "heads"), None),
            P("docs", None),
            P("docs", "heads"),
            P("docs", "heads"),
            P("docs", "heads"),
            P("heads", "docs"),
            P("docs", "heads"),
            P("heads", "docs"),
            P("heads"),
            P("heads"),
            P(),
            P("heads"),
            P(),
            P(),
            P(),
            P(),
            P(),
        ),
        check_vma=False,
    )
```

profile of v0, /device:TPU:0, one launch (start us, length us, event | category | flops | bytes accessed | tf_op | source)
XLA Modules:
  0.0 813.4 jit_solution(10088809926398011848)
XLA Ops:
  13.6 35.0 %all_gather.21 = bf16[192,768]{0,1:T(8,128)(2,1)} all-gather(bf16[192,96]{0,1:T(8,128)(2,1)S(1)} %copy.73), channel_id=1, replica_groups=mesh['docs'=8,'heads'=4] {'docs'}, dimensions={1}, use_global_device_ids=true | all-gather | bytes 331776 | tf_op jit(solution)/shard_map/all_gather | solution.py:135
  48.5 31.3 %all_gather.18 = bf16[768,192]{1,0:T(8,128)(2,1)S(1)} all-gather(bf16[96,192]{1,0:T(8,128)(2,1)S(1)} %convert_element_type.211), channel_id=1, replica_groups=mesh['docs'=8,'heads'=4] {'docs'}, dimensions={0}, use_global_device_ids=true | all-gather | bytes 331776 | tf_op jit(solution)/shard_map/all_gather | solution.py:134
  79.8 31.2 %all_gather.20 = bf16[768,192]{1,0:T(8,128)(2,1)S(1)} all-gather(bf16[96,192]{1,0:T(8,128)(2,1)S(1)} %convert_element_type.215), channel_id=1, replica_groups=mesh['docs'=8,'heads'=4] {'docs'}, dimensions={0}, use_global_device_ids=true | all-gather | bytes 331776 | tf_op jit(solution)/shard_map/all_gather | solution.py:133
  111.0 33.0 %all_gather.19 = bf16[768,192]{1,0:T(8,128)(2,1)} all-gather(bf16[96,192]{1,0:T(8,128)(2,1)S(1)} %convert_element_type.213), channel_id=1, replica_groups=mesh['docs'=8,'heads'=4] {'docs'}, dimensions={0}, use_global_device_ids=true | all-gather | bytes 331776 | tf_op jit(solution)/shard_map/all_gather | solution.py:132
  155.4 9.9 %while.26 = (s32[]{:T(128)}, bf16[2,640,3,64]{1,3,2,0:T(8,128)(2,1)S(1)}, f32[2,3,640]{2,1,0:T(4,128)S(1)}, bf16[2,640,3,64]{1,3,2,0:T(8,128)(2,1)S(1)}, s32[2]{...) while((s32[]{:T(128)}, ...), condition=%wide.region_4.5_spmd, body=%wide.region_1.4_spmd.sunk | while | flops 329440000 | bytes 15808389 | solution.py:165
  165.9 2.7 fusion.97
  170.7 80.0 %all-reduce.6.cloned.1.call-done = f32[1280,768]{1,0:T(8,128)} async-done(((f32[1280,768]{1,0:T(8,128)}), f32[1280,768]{1,0:T(8,128)}) %all-reduce.6.cloned.1.call-update) | async-done | bytes 3932176 | tf_op jit(solution)/shard_map/psum | solution.py:170
  250.6 3.8 fusion.96
  258.6 12.9 %multiply_convert_fusion.1 = (bf16[1280,768]{1,0:T(8,128)(2,1)S(1)}, f32[1280,768]{1,0:T(8,128)}, f32[1280,768]{1,0:T(8,128)}) fusion(f32[768]{0:T(1024)S(1)} %copy-done.55, bf16[768,768]{1,0:T(8,128)(2,1)} %all-gather.3.cloned.1.call-done, f32[1280,768]{1,0:T(8,128)} %subtract_multiply_fusion.3, f32[768]{0:T(1024)S(1)} %copy-done.42, f32[768]{0:T(1024)S(1)} %copy-done.39), kind=kOutput, calls=%fused_computation.81 | convolution fusion | flops 1577779200 | bytes 14951424 | tf_op jit(solution)/shard_map/dot_general | solution.py:174
  271.6 5.0 convolution_convert_fusion.1
  276.8 49.3 %all-reduce.8.cloned.1.call-done = bf16[1280,768]{1,0:T(8,128)(2,1)} async-done(((bf16[1280,768]{1,0:T(8,128)(2,1)}), bf16[1280,768]{1,0:T(8,128)(2,1)}) %all-reduce.8.cloned.1.call-update) | async-done | bytes 1966096 | tf_op jit(solution)/shard_map/psum | solution.py:177
  326.1 3.8 fusion.91
  332.8 2.6 multiply_reduce_fusion.6
  340.0 2.7 convert_reduce_fusion
  344.0 3.0 convolution_convert_fusion
  347.1 3.6 fusion.92
  350.7 45.8 %all-reduce.10.cloned.1.call-done = bf16[1280,768]{1,0:T(8,128)(2,1)} async-done(((bf16[1280,768]{1,0:T(8,128)(2,1)}), bf16[1280,768]{1,0:T(8,128)(2,1)}) %all-reduce.10.cloned.1.call-update) | async-done | bytes 1966096 | tf_op jit(solution)/shard_map/psum | solution.py:195
  396.5 6.7 multiply_reduce_fusion.5
  416.5 18.4 %while.27 = (s32[]{:T(128)}, bf16[2,640,3,64]{1,3,2,0:T(8,128)(2,1)}, bf16[2,640,3,64]{1,3,2,0:T(8,128)(2,1)}, bf16[2,640,3,64]{1,3,2,0:T(8,128)(2,1)}, bf16[2,6...) while((s32[]{:T(128)}, ...), condition=%wide.region_18.19_spmd, body=%wide.region_16.18_spmd.sunk | while | flops 805477120 | bytes 53151840 | solution.py:204
  437.3 3.1 convolution_convert_fusion.8
  444.1 3.1 convolution_convert_fusion.7
  447.2 3.7 fusion.98
  451.2 3.1 convolution_add_fusion.1
  456.4 4.9 convolution_convert_fusion.4
  461.4 5.8 convolution_convert_fusion.5
  476.9 41.3 %all-reduce = (f32[768]{0:T(1024)S(1)}, f32[768]{0:T(1024)S(1)}, f32[768]{0:T(1024)}, f32[3072]{0:T(1024)S(1)}, f32[768]{0:T(1024)}, /*index=5*/f32[768]{0:T(1024)}, f32[768]{0:T(1024)}, f32[768]{0:T(1024)}, f32[768]{0:T(1024)}) all-reduce(f32[768]{0:T(1024)S(1)} %dynamic_update_slice.26, ...), channel_id=1, replica_groups=mesh['docs'=8,'heads'=4] {'docs','heads'}, use_global_device_ids=true, to_apply=%region_27.28 | all-reduce | flops 9216 | bytes 73728 | tf_op jit(solution)/shard_map/psum | solution.py:290
  521.8 19.2 %reduce-scatter.9.cloned.1.call-done = bf16[96,192]{1,0:T(8,128)(2,1)} async-done(((bf16[768,192]{1,0:T(8,128)(2,1)}), bf16[96,192]{1,0:T(8,128)(2,1)}) %reduce-scatter.9.cloned.1.call-update) | async-done | bytes 36880 | tf_op jit(solution)/shard_map/reduce_scatter | solution.py:256
  542.4 63.1 %reduce-scatter.13.cloned.1.call-done = bf16[96,192]{1,0:T(8,128)(2,1)} async-done(((bf16[768,192]{1,0:T(8,128)(2,1)}), bf16[96,192]{1,0:T(8,128)(2,1)}) %reduce-scatter.13.cloned.1.call-update) | async-done | bytes 36880 | tf_op jit(solution)/shard_map/reduce_scatter | solution.py:262
  606.9 63.1 %reduce-scatter.11.cloned.1.call-done = bf16[96,192]{1,0:T(8,128)(2,1)} async-done(((bf16[768,192]{1,0:T(8,128)(2,1)}), bf16[96,192]{1,0:T(8,128)(2,1)}) %reduce-scatter.11.cloned.1.call-update) | async-done | bytes 36880 | tf_op jit(solution)/shard_map/reduce_scatter | solution.py:259
  671.5 4.6 add_convert_fusion
  680.1 57.0 %reduce-scatter.17.cloned.1.call-done = bf16[768,96]{0,1:T(8,128)(2,1)} async-done(((bf16[768,768]{0,1:T(8,128)(2,1)}), bf16[768,96]{0,1:T(8,128)(2,1)}) %reduce-scatter.17.cloned.1.call-update) | async-done | bytes 147472 | tf_op jit(solution)/shard_map/reduce_scatter | solution.py:271
  738.8 65.4 %reduce-scatter.15.cloned.1.call-done = bf16[96,768]{1,0:T(8,128)(2,1)} async-done(((bf16[768,768]{1,0:T(8,128)(2,1)}), bf16[96,768]{1,0:T(8,128)(2,1)}) %reduce-scatter.15.cloned.1.call-update) | async-done | bytes 147472 | tf_op jit(solution)/shard_map/reduce_scatter | solution.py:268
  (277 shorter events, 104.0 us)
Async XLA Ops:
  8.0 137.7 %copy-start.45 = (s32[2,512]{1,0:T(2,128)S(1)}, s32[2,512]{1,0:T(2,128)}, u32[]{:S(2)}) copy-start(s32[2,512]{1,0:T(2,128)} %param.24) | copy-start | bytes 12292
  8.0 137.7 %copy-start.36 = (bf16[1280,768]{1,0:T(8,128)(2,1)S(1)}, bf16[1280,768]{1,0:T(8,128)(2,1)}, u32[]{:S(2)}) copy-start(bf16[1280,768]{1,0:T(8,128)(2,1)} %param.23) | copy-start | bytes 5898244
  8.0 242.6 %all-reduce.6.cloned.1.call-start = ((), (), s32[]{:S(2)}) async-start(), calls=%async_computation.6 | async-start | bytes 7864320 | tf_op jit(solution)/shard_map/psum | solution.py:170
  9.0 137.6 %copy-start.51 = (f32[2,128]{1,0:T(2,128)}, f32[2,128]{1,0:T(2,128)S(1)}, u32[]{:S(2)}) copy-start(f32[2,128]{1,0:T(2,128)S(1)} %compare_convert_fusion) | copy-start | bytes 3076
  9.9 136.7 %copy-start.49 = (f32[2,128]{1,0:T(2,128)}, f32[2,128]{1,0:T(2,128)S(1)}, u32[]{:S(2)}) copy-start(f32[2,128]{1,0:T(2,128)S(1)} %broadcast_maximum_fusion) | copy-start | bytes 3076
  79.8 72.5 %copy-start.21 = (bf16[768,192]{1,0:T(8,128)(2,1)}, bf16[768,192]{1,0:T(8,128)(2,1)S(1)}, u32[]{:S(2)}) copy-start(bf16[768,192]{1,0:T(8,128)(2,1)S(1)} %all_gather.18) | copy-start | bytes 884740
  111.0 38.4 %copy-start.19 = (bf16[768,192]{1,0:T(8,128)(2,1)}, bf16[768,192]{1,0:T(8,128)(2,1)S(1)}, u32[]{:S(2)}) copy-start(bf16[768,192]{1,0:T(8,128)(2,1)S(1)} %all_gather.20) | copy-start | bytes 884740
  155.4 10.5 %copy-start.24 = (bf16[192,768]{0,1:T(8,128)(2,1)S(1)}, bf16[192,768]{0,1:T(8,128)(2,1)}, u32[]{:S(2)}) copy-start(bf16[192,768]{0,1:T(8,128)(2,1)} %all_gather.21) | copy-start | bytes 884740
  165.9 84.7 %copy-start.43 = (f32[768]{0:T(1024)S(1)}, f32[768]{0:T(1024)}, u32[]{:S(2)}) copy-start(f32[768]{0:T(1024)} %param.34) | copy-start | bytes 9220
  168.6 90.0 %all-gather.3.cloned.1.call-start = ((), (), s32[]{:S(2)}) async-start(), calls=%async_computation.7 | async-start | bytes 1327104 | tf_op jit(solution)/shard_map/all_gather | solution.py:136
  169.4 102.2 %all-gather.5.cloned.1.call-start = ((), (), s32[]{:S(2)}) async-start(), calls=%async_computation.8 | async-start | bytes 1327104 | tf_op jit(solution)/shard_map/all_gather | solution.py:137
  170.2 156.0 %all-reduce.8.cloned.1.call-start = ((), (), s32[]{:S(2)}) async-start(), calls=%async_computation.9 | async-start | bytes 3932160 | tf_op jit(solution)/shard_map/psum | solution.py:177
  271.6 5.0 copy-start.58
  271.6 54.5 %copy-start.41 = (f32[768]{0:T(1024)S(1)}, f32[768]{0:T(1024)}, u32[]{:S(2)}) copy-start(f32[768]{0:T(1024)} %param.36) | copy-start | bytes 9220
  276.6 119.9 %all-reduce.10.cloned.1.call-start = ((), (), s32[]{:S(2)}) async-start(), calls=%async_computation.10 | async-start | bytes 3932160 | tf_op jit(solution)/shard_map/psum | solution.py:195
  326.1 3.9 copy-start.1
  326.1 4.5 copy-start.9
  332.7 4.6 copy-start.60
  335.4 4.6 copy-start.59
  337.3 5.4 copy-start.27
  340.0 4.0 copy-start.53
  347.0 173.2 %reduce-scatter.19.cloned.1.call-start = ((), (), s32[]{:S(2)}) async-start(), calls=%async_computation.17 | async-start | bytes 442368
  396.5 6.7 copy-start.2
  413.8 127.2 %reduce-scatter.9.cloned.1.call-start = ((), (), s32[]{:S(2)}) async-start(), calls=%async_computation.12 | async-start | bytes 442368 | tf_op jit(solution)/shard_map/reduce_scatter | solution.py:256
  434.9 5.6 copy-start.35
  440.5 165.0 %reduce-scatter.13.cloned.1.call-start = ((), (), s32[]{:S(2)}) async-start(), calls=%async_computation.14 | async-start | bytes 442368 | tf_op jit(solution)/shard_map/reduce_scatter | solution.py:262
  444.0 226.0 %reduce-scatter.11.cloned.1.call-start = ((), (), s32[]{:S(2)}) async-start(), calls=%async_computation.13 | async-start | bytes 442368 | tf_op jit(solution)/shard_map/reduce_scatter | solution.py:259
  447.1 4.1 copy-start.20
  450.9 220.6 %all-reduce.12.cloned.1.call-start = ((), (), s32[]{:S(2)}) async-start(), calls=%async_computation.11 | async-start | bytes 3932160 | tf_op jit(solution)/shard_map/psum | solution.py:230
  456.4 280.8 %reduce-scatter.17.cloned.1.call-start = ((), (), s32[]{:S(2)}) async-start(), calls=%async_computation.16 | async-start | bytes 1327104 | tf_op jit(solution)/shard_map/reduce_scatter | solution.py:271
  461.4 342.8 %reduce-scatter.15.cloned.1.call-start = ((), (), s32[]{:S(2)}) async-start(), calls=%async_computation.15 | async-start | bytes 1327104 | tf_op jit(solution)/shard_map/reduce_scatter | solution.py:268
  467.3 6.2 copy-start.18
  (48 other events, 100.2 us)
Sparse Core Ops, SparseCore 0:
  168.7 81.8 all-reduce.5
  276.7 49.3 all-reduce.7
  347.1 49.3 all-reduce.9
  456.5 49.4 all-reduce.11
Sparse Core Ops, SparseCore 1:
  171.9 41.8 all-gather.2
  216.4 39.5 all-gather.4
  413.9 62.3 reduce-scatter.18
  479.5 61.4 reduce-scatter.8
  544.2 61.2 reduce-scatter.12
  608.8 61.2 reduce-scatter.10
  673.3 63.8 reduce-scatter.16
  740.4 63.7 reduce-scatter.14
where the time goes:
time: 821 us; the launch traced here: 813 us
  waiting for transfers between devices  443 us (54%)
  blocking collectives  172 us (21%)
  matrix products  79 us (10%)
  other arithmetic  64.9 us (8%)
  local copies, waits for them, and re-layouts  33.5 us (4%)
  between operations  16.6 us (2%)
    psum x1, waiting for transfers between devices, body(): attn_total = lax.psum(attn_part, 'heads')  80 us
    reduce_scatter x1, waiting for transfers between devices, body(): lax.psum_scatter(grad_weight_up.astype(jnp.bfloat16), 'docs', scatter_dim...  65.4 us
    reduce_scatter x1, waiting for transfers between devices, body(): lax.psum_scatter(grad_weight_value.astype(jnp.bfloat16), 'docs', scatter_...  63.1 us
    reduce_scatter x1, waiting for transfers between devices, body(): lax.psum_scatter(grad_weight_key.astype(jnp.bfloat16), 'docs', scatter_di...  63.1 us
    reduce_scatter x1, waiting for transfers between devices, body(): lax.psum_scatter(grad_weight_down.astype(jnp.bfloat16), 'docs', scatter_d...  57 us
    psum x1, waiting for transfers between devices, body(): lax.psum(down_part.astype(jnp.bfloat16), 'heads').astype(jnp.float32)  49.3 us
    psum x1, waiting for transfers between devices, body(): lax.psum(grad_normed_part.astype(jnp.bfloat16), 'heads').astype(jnp.float32)  45.8 us
    psum x1, blocking collectives, body(): lax.psum((widen(bias_query_part), widen(bias_value_part), widen(bias_up_p...  41.3 us
  transfers between devices with their start and end apart: 12, of which 8 were waited for; matrix products, arithmetic and copies ran while one was open for 12% of the time, Pallas kernels for 0%

commit v1 on v0

v1 whole, which is shorter than its diff:
```python
from functools import partial

import jax
import jax.numpy as jnp
from jax import lax
from jax.sharding import PartitionSpec as P

HEAD_DIM = 64


epsilon = 1e-05
masked_score = -1000000000.0


def norm_forward(pre_rows, gain_vec, shift_vec):
    average = jnp.mean(pre_rows, axis=-1, keepdims=True)
    centered = pre_rows - average
    variance = jnp.mean(centered * centered, axis=-1, keepdims=True)
    inv_std = lax.rsqrt(variance + epsilon)
    scaled = centered * inv_std
    return (scaled * gain_vec + shift_vec, scaled, inv_std)


def norm_backward(grad_out, scaled, inv_std, gain_vec):
    grad_scaled = grad_out * gain_vec
    mean_grad = jnp.mean(grad_scaled, axis=-1, keepdims=True)
    mean_along = jnp.mean(grad_scaled * scaled, axis=-1, keepdims=True)
    return inv_std * (grad_scaled - mean_grad - scaled * mean_along)


def contract_rows(left_side, right_side):
    return lax.dot_general(
        left_side, right_side, (((0,), (0,)), ((), ())), preferred_element_type=jnp.float32
    )


def contract_cols(left_side, right_side):
    return lax.dot_general(
        left_side, right_side, (((1,), (1,)), ((), ())), preferred_element_type=jnp.float32
    )


def score_block(queries, key_rows, seg_total, text_len):
    score_scale = HEAD_DIM ** (-0.5)
    scores = (
        jnp.einsum("hqd,hkd->hqk", queries, key_rows, preferred_element_type=jnp.float32)
        * score_scale
    )
    visible = jnp.arange(key_rows.shape[1], dtype=jnp.int32) < text_len + seg_total
    return jnp.where(visible[None, None, :], scores, masked_score)


def attend_forward(text_len, queries, key_rows, value_rows, seg_total):
    scores = score_block(queries, key_rows, seg_total, text_len)
    top_score = jnp.max(scores, axis=-1, keepdims=True)
    raised = jnp.exp(scores - top_score)
    totals = jnp.sum(raised, axis=-1, keepdims=True)
    probs_low = (raised / totals).astype(jnp.bfloat16)
    context = jnp.einsum("hqk,hkd->hqd", probs_low, value_rows, preferred_element_type=jnp.float32)
    return context.astype(jnp.bfloat16), top_score + jnp.log(totals)


def attend_backward(text_len, queries, key_rows, value_rows, seg_total, log_total, grad_context):
    scores = score_block(queries, key_rows, seg_total, text_len)
    attn_probs = jnp.exp(scores - log_total)
    grad_probs = jnp.einsum(
        "hqd,hkd->hqk", grad_context, value_rows, preferred_element_type=jnp.float32
    )
    inner_sum = jnp.sum(grad_probs * attn_probs, axis=-1, keepdims=True)
    grad_scores = (attn_probs * (grad_probs - inner_sum)).astype(jnp.bfloat16)
    score_scale = HEAD_DIM ** (-0.5)
    grad_values = jnp.einsum(
        "hqk,hqd->hkd",
        attn_probs.astype(jnp.bfloat16),
        grad_context,
        preferred_element_type=jnp.float32,
    )
    grad_queries = (
        jnp.einsum("hqk,hkd->hqd", grad_scores, key_rows, preferred_element_type=jnp.float32)
        * score_scale
    )
    grad_keys = (
        jnp.einsum("hqk,hqd->hkd", grad_scores, queries, preferred_element_type=jnp.float32)
        * score_scale
    )
    return (
        grad_queries.astype(jnp.bfloat16),
        grad_keys.astype(jnp.bfloat16),
        grad_values.astype(jnp.bfloat16),
    )


def flip_perm(size, bit):
    return [(at, at ^ bit) for at in range(size)]


def body(
    tokens,
    seg_index,
    seg_count,
    weight_query,
    weight_key,
    weight_value,
    weight_out,
    weight_up,
    weight_down,
    bias_query,
    bias_value,
    bias_out,
    bias_up,
    bias_down,
    gain_one,
    shift_one,
    gain_two,
    shift_two,
    cotangent,
):
    low, full = jnp.bfloat16, jnp.float32
    width = tokens.shape[1]
    text_len = seg_index.shape[1]
    seq_len = tokens.shape[0] // seg_count.shape[0]
    slot_total = seq_len - text_len
    half = seq_len // 2
    docs_size = lax.axis_size("docs")
    stages = docs_size.bit_length() - 1
    docs_pos = lax.axis_index("docs")
    heads_pos = lax.axis_index("heads")
    core = heads_pos % 2
    side = heads_pos // 2
    slab = weight_query.shape[1]
    block = weight_query.shape[0]
    hidden = weight_up.shape[1]

    def swap_core(array):
        return lax.ppermute(array, "heads", flip_perm(4, 1))

    def swap_side(array):
        return lax.ppermute(array, "heads", flip_perm(4, 2))

    def swap_docs(array, stage):
        return lax.ppermute(array, "docs", flip_perm(docs_size, 1 << stage))

    def docs_bit(stage):
        return (docs_pos >> stage) & 1

    def join(own, got, bit, axis):
        return jnp.stack([jnp.where(bit == 0, own, got), jnp.where(bit == 0, got, own)], axis)

    def gather_far(shard):
        out = shard
        for step, stage in enumerate(range(stages - 1, 0, -1)):
            out = join(out, swap_docs(out, stage), docs_bit(stage), step)
        return out.reshape((docs_size // 2,) + shard.shape)

    def gather_near(part):
        return join(part, swap_docs(part, 0), docs_bit(0), 1).reshape(
            (docs_size,) + part.shape[1:]
        )

    def gather_side(part):
        return join(part, swap_side(part), side, 0)

    shard_attn = jnp.concatenate(
        [weight_query, weight_key, weight_value, weight_out.T], axis=1
    ).astype(low)
    shard_ffn = jnp.concatenate([weight_up, weight_down.T], axis=1).astype(low)
    far_attn = gather_far(shard_attn)
    shard_ffn, far_attn = lax.optimization_barrier((shard_ffn, far_attn))
    far_ffn = gather_far(shard_ffn)
    pair = 2 * slab
    qk_full = gather_side(gather_near(far_attn[..., :pair])).reshape(2, width, pair)
    vo_side = gather_side(far_attn[..., pair:])
    vo_full = join(vo_side, swap_docs(vo_side, 0), docs_bit(0), 2).reshape(2, width, pair)
    up_full = gather_side(gather_near(far_ffn[..., :hidden])).reshape(2, width, hidden)
    down_side = gather_side(far_ffn[..., hidden:])
    down_full = join(down_side, swap_docs(down_side, 0), docs_bit(0), 2).reshape(2, width, hidden)

    bias_sides = jnp.concatenate([bias_query, bias_value, bias_up])
    bias_sides = join(bias_sides, swap_side(bias_sides), side, 0)
    query_bias = bias_sides[:, :slab]
    value_bias = bias_sides[:, slab:pair]
    hidden_bias = bias_sides[:, pair:]

    doc = lax.dynamic_index_in_dim(tokens.reshape(2, seq_len, width), side, 0, keepdims=False)
    doc_index = lax.dynamic_index_in_dim(seg_index, side, 0, keepdims=False)
    doc_count = lax.dynamic_index_in_dim(seg_count, side, 0, keepdims=False)
    row_start = core * half

    def my_rows(array):
        return lax.dynamic_slice_in_dim(array, row_start, half, 0)

    def reduce_core(part):
        theirs = lax.dynamic_slice_in_dim(part, (1 - core) * half, half, 0).astype(low)
        return my_rows(part) + swap_core(theirs).astype(full)

    def gather_core(rows):
        return join(rows, swap_core(rows), core, 0).reshape(seq_len, width)

    slot_ids = jnp.arange(slot_total, dtype=jnp.int32)
    onehot = (doc_index[:, None] == slot_ids[None, :]).astype(low)
    members = jnp.sum(onehot.astype(full), axis=0)
    divisor = jnp.maximum(members, 1.0)[:, None]
    text_rows = doc[:text_len]
    pooled = contract_rows(onehot, text_rows) / divisor
    slot_live = (slot_ids < doc_count).astype(full)[:, None]
    slot_rows = slot_live * (doc[text_len:].astype(full) + pooled)
    inputs = jnp.concatenate([text_rows.astype(full), slot_rows], axis=0)
    hidden_in = inputs.astype(low)

    def project(weight, bias):
        out = jnp.einsum("rd,sde->sre", hidden_in, weight, preferred_element_type=full)
        return out + bias[:, None, :]

    qk_rows = project(
        qk_full, jnp.concatenate([query_bias, jnp.zeros_like(query_bias)], axis=1)
    ).astype(low)
    v_rows = project(vo_full[..., :slab], value_bias).astype(low)
    out_full = vo_full[..., slab:]
    heads_slab = slab // HEAD_DIM

    def to_heads(array):
        return (
            array.reshape(2, seq_len, heads_slab, HEAD_DIM)
            .transpose(0, 2, 1, 3)
            .reshape(2 * heads_slab, seq_len, HEAD_DIM)
        )

    def from_heads(array):
        return (
            array.reshape(2, heads_slab, seq_len, HEAD_DIM)
            .transpose(0, 2, 1, 3)
            .reshape(2, seq_len, slab)
        )

    query_heads = to_heads(qk_rows[..., :slab])
    key_heads = to_heads(qk_rows[..., slab:])
    value_heads = to_heads(v_rows)
    context_heads, log_total = attend_forward(
        text_len, query_heads, key_heads, value_heads, doc_count
    )
    context = from_heads(context_heads)
    attn_part = jnp.einsum("src,sdc->rd", context, out_full, preferred_element_type=full)
    pre_one = my_rows(inputs) + (reduce_core(attn_part) + bias_out)
    normed_one, scaled_one, inv_one = norm_forward(pre_one, gain_one, shift_one)
    normed_low = gather_core(normed_one.astype(low))
    upward = (
        jnp.einsum("rd,sdh->srh", normed_low, up_full, preferred_element_type=full)
        + hidden_bias[:, None, :]
    )
    activated = jax.nn.gelu(upward, approximate=False).astype(low)
    down_part = jnp.einsum("srh,sdh->rd", activated, down_full, preferred_element_type=full)
    grad_rows_out = lax.dynamic_slice_in_dim(
        cotangent, side * seq_len + row_start, half, 0
    ).astype(full)
    pre_two = normed_one + (reduce_core(down_part) + bias_down)
    normed_two, scaled_two, inv_two = norm_forward(pre_two, gain_two, shift_two)
    layer_out = normed_two.astype(low)
    grad_pre_two = norm_backward(grad_rows_out, scaled_two, inv_two, gain_two)
    gain_two_part = jnp.sum(grad_rows_out * scaled_two, axis=0)
    shift_two_part = jnp.sum(grad_rows_out, axis=0)
    grad_down_half = grad_pre_two.astype(low)
    bias_down_part = jnp.sum(grad_down_half.astype(full), axis=0)
    grad_down_low = gather_core(grad_down_half)
    grad_weight_down = jnp.einsum(
        "rd,srh->sdh", grad_down_low, activated, preferred_element_type=full
    )
    grad_activated = jnp.einsum(
        "rd,sdh->srh", grad_down_low, down_full, preferred_element_type=full
    )
    gelu_value, gelu_back = jax.vjp(partial(jax.nn.gelu, approximate=False), upward)
    grad_up_low = gelu_back(grad_activated)[0].astype(low)
    grad_weight_up = jnp.einsum("rd,srh->sdh", normed_low, grad_up_low, preferred_element_type=full)
    bias_up_part = jnp.sum(grad_up_low.astype(full), axis=1)
    grad_normed_part = jnp.einsum(
        "srh,sdh->rd", grad_up_low, up_full, preferred_element_type=full
    )
    grad_normed = reduce_core(grad_normed_part) + grad_pre_two
    grad_pre_one = norm_backward(grad_normed, scaled_one, inv_one, gain_one)
    gain_one_part = jnp.sum(grad_normed * scaled_one, axis=0)
    shift_one_part = jnp.sum(grad_normed, axis=0)
    grad_branch_half = grad_pre_one.astype(low)
    bias_out_part = jnp.sum(grad_branch_half.astype(full), axis=0)
    grad_branch_low = gather_core(grad_branch_half)
    grad_weight_out = jnp.einsum(
        "rd,src->sdc", grad_branch_low, context, preferred_element_type=full
    )
    grad_context = jnp.einsum(
        "rd,sdc->src", grad_branch_low, out_full, preferred_element_type=full
    ).astype(low)
    grad_q_heads, grad_k_heads, grad_v_heads = attend_backward(
        text_len,
        query_heads,
        key_heads,
        value_heads,
        doc_count,
        log_total,
        to_heads(grad_context),
    )
    grad_qk = jnp.concatenate([from_heads(grad_q_heads), from_heads(grad_k_heads)], axis=2)
    grad_v = from_heads(grad_v_heads)
    grad_weight_qk = jnp.einsum("rd,src->sdc", hidden_in, grad_qk, preferred_element_type=full)
    grad_weight_v = jnp.einsum("rd,src->sdc", hidden_in, grad_v, preferred_element_type=full)
    bias_query_part = jnp.sum(grad_qk[..., :slab].astype(full), axis=1)
    bias_value_part = jnp.sum(grad_v.astype(full), axis=1)
    grad_hidden_part = jnp.einsum(
        "src,sdc->rd", grad_qk, qk_full, preferred_element_type=full
    ) + jnp.einsum("src,sdc->rd", grad_v, vo_full[..., :slab], preferred_element_type=full)
    grad_inputs = (reduce_core(grad_hidden_part) + grad_pre_one).astype(low)
    grad_sides = join(grad_inputs, swap_side(grad_inputs), side, 0)
    grad_all = join(grad_sides, swap_core(grad_sides), core, 1).reshape(2, seq_len, width)
    grad_all = lax.optimization_barrier(grad_all).astype(full)
    onehot_both = (seg_index[:, :, None] == slot_ids[None, None, :]).astype(full)
    divisor_both = jnp.maximum(jnp.sum(onehot_both, axis=1), 1.0)[:, :, None]
    live_both = (slot_ids[None, :] < seg_count[:, None]).astype(full)[:, :, None]
    grad_slots = live_both * grad_all[:, text_len:]
    spread_back = jnp.einsum(
        "gts,gsd->gtd",
        onehot_both,
        grad_slots / divisor_both,
        precision=lax.Precision.HIGHEST,
        preferred_element_type=full,
    )
    grad_tokens = (
        jnp.concatenate([grad_all[:, :text_len] + spread_back, grad_slots], axis=1)
        .reshape(2 * seq_len, width)
        .astype(low)
    )

    def scatter_side(parts):
        theirs = lax.dynamic_index_in_dim(parts, 1 - side, 0, keepdims=False).astype(low)
        mine = lax.dynamic_index_in_dim(parts, side, 0, keepdims=False)
        return mine + swap_side(theirs).astype(full)

    def scatter_docs(parts, stage, axis):
        bit = docs_bit(stage)
        theirs = lax.dynamic_index_in_dim(parts, 1 - bit, axis, keepdims=False).astype(low)
        mine = lax.dynamic_index_in_dim(parts, bit, axis, keepdims=False)
        return mine + swap_docs(theirs, stage).astype(full)

    def scatter_far(parts):
        out = parts.reshape((2,) * (stages - 1) + parts.shape[1:])
        for stage in range(1, stages):
            out = scatter_docs(out, stage, stages - 1 - stage)
        return out

    def scatter_weights(first, second):
        cut = (2, docs_size // 2, 2, block, first.shape[-1])
        first = scatter_side(scatter_docs(first.reshape(cut), 0, 2))
        second = scatter_docs(scatter_side(second.reshape(cut)), 0, 1)
        return scatter_far(jnp.concatenate([first, second], axis=-1))

    total_ffn = scatter_weights(grad_weight_up, grad_weight_down)
    total_attn = scatter_weights(
        grad_weight_qk, jnp.concatenate([grad_weight_v, grad_weight_out], axis=-1)
    )

    def widen(part_sides):
        wide = jnp.zeros((2, 2, part_sides.shape[1]), full)
        return lax.dynamic_update_slice(wide, part_sides[:, None, :], (0, core, 0)).reshape(-1)

    (
        wide_query,
        wide_value,
        wide_up,
        gradient_bias_out,
        gradient_bias_down,
        gradient_gain_one,
        gradient_shift_one,
        gradient_gain_two,
        gradient_shift_two,
    ) = lax.psum(
        (
            widen(bias_query_part),
            widen(bias_value_part),
            widen(bias_up_part),
            bias_out_part,
            bias_down_part,
            gain_one_part,
            shift_one_part,
            gain_two_part,
            shift_two_part,
        ),
        ("docs", "heads"),
    )

    def own_share(wide, size):
        return lax.dynamic_slice_in_dim(wide, heads_pos * size, size, 0)

    return (
        layer_out,
        grad_tokens,
        total_attn[:, :slab],
        total_attn[:, slab:pair],
        total_attn[:, pair : pair + slab],
        total_attn[:, pair + slab :].T,
        total_ffn[:, :hidden],
        total_ffn[:, hidden:].T,
        own_share(wide_query, slab),
        own_share(wide_value, slab),
        gradient_bias_out,
        own_share(wide_up, hidden),
        gradient_bias_down,
        gradient_gain_one,
        gradient_shift_one,
        gradient_gain_two,
        gradient_shift_two,
    )


def solution(mesh):
    placed = (
        P("docs", None),
        P("docs", None),
        P("docs"),
        P("docs", "heads"),
        P("docs", "heads"),
        P("docs", "heads"),
        P("heads", "docs"),
        P("docs", "heads"),
        P("heads", "docs"),
        P("heads"),
        P("heads"),
        P(),
        P("heads"),
        P(),
        P(),
        P(),
        P(),
        P(),
        P("docs", None),
    )
    return jax.shard_map(
        body,
        mesh=mesh,
        in_specs=placed,
        out_specs=(
            P(("docs", "heads"), None),
            P("docs", None),
            P("docs", "heads"),
            P("docs", "heads"),
            P("docs", "heads"),
            P("heads", "docs"),
            P("docs", "heads"),
            P("heads", "docs"),
            P("heads"),
            P("heads"),
            P(),
            P("heads"),
            P(),
            P(),
            P(),
            P(),
            P(),
        ),
        check_vma=False,
    )
```

time: 821 us -> 376 us (0.46)
  waiting for transfers between devices: 443 us -> 107 us
  blocking collectives: 172 us -> 50.3 us
  starting transfers between devices: 1.61 us -> 36.3 us
  between operations: 16.6 us -> 3.04 us
  local copies, waits for them, and re-layouts: 33.5 us -> 46.9 us
  matrix products: 79 us -> 68.5 us
    reduce_scatter x5 -> x0, waiting for transfers between devices: 268 us -> none  [the longest x1 65.4 us: body(): lax.psum_scatter(grad_weight_up.astype(jnp.bfloat16), 'docs', scatter_dim...]
    psum x4 -> x0, waiting for transfers between devices: 175 us -> none  [the longest x1 80 us: body(): attn_total = lax.psum(attn_part, 'heads')]
    all_gather x4 -> x0, blocking collectives: 130 us -> none  [the longest x1 35 us: body(): lax.all_gather(weight_out.astype(jnp.bfloat16), 'docs', axis=1, tiled=True)]
    ppermute x0 -> x34, waiting for transfers between devices: none -> 107 us  [the longest x16 82.4 us: swap_docs(): return lax.ppermute(array, 'docs', flip_perm(docs_size, 1 << stage))]
    ppermute x0 -> x34, starting transfers between devices: none -> 36.3 us  [the longest x16 22.7 us: swap_docs(): return lax.ppermute(array, 'docs', flip_perm(docs_size, 1 << stage))]
    convert_element_type x19 -> x7, other arithmetic: 28 us -> 3.52 us  [the longest x1 1.25 us: body(): inputs = jnp.concatenate([text_rows.astype(full), slot_rows], axis=0)]
    dot_general x6 -> x1, matrix products: 19.7 us -> 0.41 us  [contract_rows(): lax.dot_general(left_side, right_side, (((0,), (0,)), ((), ())), preferre...]
    another operation x1 -> x36, other arithmetic: 0.11 us -> 16 us  [the longest x29 12.1 us: join(): jnp.stack([jnp.where(bit == 0, own, got), jnp.where(bit == 0, got, own)],...]
  transfers between devices with their start and end apart: 12 -> 34, of which waited for: 8 -> 19; matrix products, arithmetic and copies ran while one was open for 12% -> 34% of each run, Pallas kernels for 0% -> 0%
where the time goes in v1:
time: 376 us; the launch traced here: 370 us
  waiting for transfers between devices  107 us (28%)
  matrix products  68.5 us (18%)
  other arithmetic  57.4 us (15%)
  blocking collectives  50.3 us (13%)
  local copies, waits for them, and re-layouts  46.9 us (12%)
  starting transfers between devices  36.3 us (10%)
    ppermute x16, waiting for transfers between devices, swap_docs(): return lax.ppermute(array, 'docs', flip_perm(docs_size, 1 << stage))  82.4 us
    psum x1, blocking collectives, body(): lax.psum((widen(bias_query_part), widen(bias_value_part), widen(bias_up_p...  50.3 us
    ppermute x16, starting transfers between devices, swap_docs(): return lax.ppermute(array, 'docs', flip_perm(docs_size, 1 << stage))  22.7 us
    ppermute x10, waiting for transfers between devices, swap_side(): return lax.ppermute(array, 'heads', flip_perm(4, 2))  20.5 us
    ppermute x10, starting transfers between devices, swap_side(): return lax.ppermute(array, 'heads', flip_perm(4, 2))  12.5 us
    another operation x29, other arithmetic, join(): jnp.stack([jnp.where(bit == 0, own, got), jnp.where(bit == 0, got, own)],...  12.1 us
    unnamed x124, local copies, waits for them, and re-layouts  11.6 us
    dot_general x1, matrix products, body(): jnp.einsum('rd,sdh->srh', normed_low, up_full, preferred_element_type=full)  11.6 us
  transfers between devices with their start and end apart: 34, of which 19 were waited for; matrix products, arithmetic and copies ran while one was open for 34% of the time, Pallas kernels for 0%

profile of v1, /device:TPU:0, one launch (start us, length us, event | category | flops | bytes accessed | tf_op | source)
XLA Modules:
  0.0 369.8 jit_solution(2481460626244400507)
XLA Ops:
  1.6 3.0 collective-permute-start.4
  8.5 2.7 collective-permute-start
  23.1 6.3 %collective-permute-done.1 = bf16[2,96,768]{2,1,0:T(8,128)(2,1)} collective-permute-done((bf16[2,96,768]{2,1,0:T(8,128)(2,1)}, bf16[2,96,768]{2,1,0:T(8,128)(2,1)}, u32[]{:S(2)}, u32[]{:S(2)}) %collective-permute-start.1) | collective-permute-done | bytes 294944 | tf_op jit(solution)/shard_map/ppermute | solution.py:141
  41.6 6.6 %collective-permute-done.8 = bf16[96,1536]{1,0:T(8,128)(2,1)S(1)} collective-permute-done((bf16[96,1536]{1,0:T(8,128)(2,1)S(1)}, bf16[96,1536]{1,0:T(8,128)(2,1)S(1)}, u32[]{:S(2)}, u32[]{:S(2)}) %collective-permute-start.8) | collective-permute-done | bytes 294944 | tf_op jit(solution)/shard_map/ppermute | solution.py:141
  61.4 2.8 reshape.272
  64.2 2.4 fusion.34
  71.7 3.4 fusion.105
  76.5 2.5 copy-done
  79.0 2.4 fusion.37
  87.6 12.1 %collective-permute-done.13 = bf16[4,96,768]{2,1,0:T(8,128)(2,1)S(1)} collective-permute-done((bf16[4,96,768]{2,1,0:T(8,128)(2,1)S(1)}, bf16[4,96,768]{2,1,0:T(8,128)(2,1)S(1)}, u32[]{:S(2)}, u32[]{:S(2)}) %collective-permute-start.13) | collective-permute-done | bytes 589856 | tf_op jit(solution)/shard_map/ppermute | solution.py:138
  108.4 21.3 %collective-permute-done.14 = bf16[2,4,96,768]{3,2,1,0:T(8,128)(2,1)} collective-permute-done((bf16[2,4,96,768]{3,2,1,0:T(8,128)(2,1)}, bf16[2,4,96,768]{3,2,1,0:T(8,128)(2,1)}, u32[]{:S(2)}, u32[]{:S(2)}) %collective-permute-start.14) | collective-permute-done | bytes 1179680 | tf_op jit(solution)/shard_map/ppermute | solution.py:141
  134.9 11.6 %fusion.15 = (bf16[2,640,768]{2,1,0:T(8,128)(2,1)S(1)}, f32[2,640,768]{2,1,0:T(8,128)}, f32[2,768,640]{1,2,0:T(8,128)}) fusion(f32[2,768]{1,0:T(2,128)S(1)} %pad_maximum_fusion.35, bf16[640,768,1]{1,0,2:T(8,128)(2,1)S(1)} %bitcast.372, bf16[1,768,768]{2,1,0:T(8,128)(2,1)S(1)} %bitcast.370, bf16[1,768,768]{2,1,0:T(8,128)(2,1)S(1)} %bitcast.368), kind=kOutput, calls=%fused_computation.28 | convolution fusion | flops 1579548672 | bytes 13178880 | tf_op jit(solution)/shard_map/rd,sdh->srh/dot_general | solution.py:247
  158.6 5.2 %convert_reduce_fusion = (f32[2,768]{1,0:T(2,128)S(1)}, bf16[2,640,768]{2,1,0:T(8,128)(2,1)S(1)}) fusion(f32[2,640,768]{2,1,0:T(8,128)} %get-tuple-element.115, bf16[640,768,1]{1,0,2:T(8,128)(2,1)S(1)} %bitcast.374, bf16[2,768,768]{2,1,0:T(8,128)(2,1)S(1)} %bitcast.364, f32[2,768,640]{1,2,0:T(8,128)} %get-tuple-element.183, f32[2,768]{1,0:T(2,128)S(1)} %pad_maximum_fusion.35), kind=kOutput, calls=%fused_computation.29 | convolution fusion | flops 1526659584 | bytes 13185024 | tf_op jit(solution)/shard_map/rd,sdh->srh/dot_general | solution.py:267
  163.9 3.0 convolution_bitcast_fusion.1
  168.8 3.6 fusion.109
  175.5 2.7 multiply_reduce_fusion.1
  189.5 5.6 %fusion.38 = bf16[6,640,64]{1,2,0:T(8,128)(2,1)S(1)} fusion(f32[6,640,640]{1,2,0:T(8,128)} %copy-done, f32[6,640]{1,0:T(8,128)S(1)} %log_add_fusion, bf16[6,640,64]{1,0,2:T(8,128)(2,1)S(1)} %reshape.281), kind=kOutput, calls=%fused_computation.80 | convolution fusion | flops 319733760 | bytes 10828800 | tf_op jit(solution)/shard_map/hqk,hqd->hkd/dot_general | solution.py:72
  195.1 7.0 %multiply_reduce_fusion = (f32[6,640]{1,0:T(8,128)S(1)}, f32[6,640,640]{1,2,0:T(8,128)}) fusion(f32[6,640,640]{1,2,0:T(8,128)} %copy-done, f32[6,640]{1,0:T(8,128)S(1)} %log_add_fusion, bf16[6,640,64]{1,0,2:T(8,128)(2,1)S(1)} %copy-done.17, bf16[6,640,64]{1,0,2:T(8,128)(2,1)S(1)} %reshape.281), kind=kOutput, calls=%fused_computation.1 | convolution fusion | flops 321941760 | bytes 20674560 | tf_op jit(solution)/shard_map/hqd,hkd->hqk/dot_general | solution.py:66
  202.1 10.7 %multiply_convert_fusion = bf16[6,640,640]{1,2,0:T(8,128)(2,1)} fusion(f32[6,640,640]{1,2,0:T(8,128)} %get-tuple-element.185, f32[6,640,640]{1,2,0:T(8,128)} %copy-done, f32[6,640]{1,0:T(8,128)S(1)} %get-tuple-element.184, f32[6,640]{1,0:T(8,128)S(1)} %log_add_fusion), kind=kLoop, calls=%fused_computation | loop fusion | flops 9830400 | bytes 24606720 | tf_op jit(solution)/shard_map/convert_element_type | solution.py:70
  212.8 3.4 fusion.36
  216.8 2.5 fusion.35
  226.8 50.3 %all-reduce = (f32[768]{0:T(1024)S(1)}, f32[768]{0:T(1024)S(1)}, f32[768]{0:T(1024)}, f32[3072]{0:T(1024)S(1)}, f32[768]{0:T(1024)}, /*index=5*/f32[768]{0:T(1024)}, f32[768]{0:T(1024)}, f32[768]{0:T(1024)}, f32[768]{0:T(1024)}) all-reduce(f32[768]{0:T(1024)S(1)} %reshape.295, ...), channel_id=1, replica_groups=mesh['docs'=8,'heads'=4] {'docs','heads'}, use_global_device_ids=true, to_apply=%region_14.15 | all-reduce | flops 9216 | bytes 73728 | tf_op jit(solution)/shard_map/psum | solution.py:371
  281.3 2.8 convolution_bitcast_fusion
  286.3 2.5 fusion.55
  292.8 2.3 bitcast_add_fusion
  302.6 3.6 collective-permute-done.22
  308.4 10.5 %collective-permute-done.31 = bf16[4,96,768]{2,1,0:T(8,128)(2,1)S(1)} collective-permute-done((bf16[4,96,768]{2,1,0:T(8,128)(2,1)S(1)}, bf16[4,96,768]{2,1,0:T(8,128)(2,1)S(1)}, u32[]{:S(2)}, u32[]{:S(2)}) %collective-permute-start.31) | collective-permute-done | bytes 589856 | tf_op jit(solution)/shard_map/ppermute | solution.py:141
  320.5 4.5 %collective-permute-done.25 = bf16[4,96,384]{2,1,0:T(8,128)(2,1)S(1)} collective-permute-done((bf16[4,96,384]{2,1,0:T(8,128)(2,1)S(1)}, bf16[4,96,384]{2,1,0:T(8,128)(2,1)S(1)}, u32[]{:S(2)}, u32[]{:S(2)}) %collective-permute-start.25) | collective-permute-done | bytes 294944 | tf_op jit(solution)/shard_map/ppermute | solution.py:141
  325.1 4.3 %collective-permute-done.23 = bf16[4,96,384]{2,1,0:T(8,128)(2,1)S(1)} collective-permute-done((bf16[4,96,384]{2,1,0:T(8,128)(2,1)S(1)}, bf16[4,96,384]{2,1,0:T(8,128)(2,1)S(1)}, u32[]{:S(2)}, u32[]{:S(2)}) %collective-permute-start.23) | collective-permute-done | bytes 294944 | tf_op jit(solution)/shard_map/ppermute | solution.py:138
  330.8 10.1 %collective-permute-done.26 = bf16[2,96,768]{2,1,0:T(8,128)(2,1)S(1)} collective-permute-done((bf16[2,96,768]{2,1,0:T(8,128)(2,1)S(1)}, bf16[2,96,768]{2,1,0:T(8,128)(2,1)S(1)}, u32[]{:S(2)}, u32[]{:S(2)}) %collective-permute-start.26) | collective-permute-done | bytes 294944 | tf_op jit(solution)/shard_map/ppermute | solution.py:141
  344.2 12.2 %collective-permute-done.27 = bf16[96,768]{1,0:T(8,128)(2,1)S(1)} collective-permute-done((bf16[96,768]{1,0:T(8,128)(2,1)S(1)}, bf16[96,768]{1,0:T(8,128)(2,1)S(1)}, u32[]{:S(2)}, u32[]{:S(2)}) %collective-permute-start.27) | collective-permute-done | bytes 147488 | tf_op jit(solution)/shard_map/ppermute | solution.py:141
  357.9 4.5 %collective-permute-done.33 = bf16[96,1536]{1,0:T(8,128)(2,1)} collective-permute-done((bf16[96,1536]{1,0:T(8,128)(2,1)S(1)}, bf16[96,1536]{1,0:T(8,128)(2,1)}, u32[]{:S(2)}, u32[]{:S(2)}) %collective-permute-start.33) | collective-permute-done | bytes 294944 | tf_op jit(solution)/shard_map/ppermute | solution.py:141
  (341 shorter events, 138.3 us)
Async XLA Ops:
  1.6 21.5 %collective-permute-start.4 = (f32[1152]{0:T(1024)S(1)}, f32[1152]{0:T(1024)S(1)}, u32[]{:S(2)}, u32[]{:S(2)}) collective-permute-start(f32[1152]{0:T(1024)S(1)} %concatenate.50), channel_id=1, source_target_pairs={{0,2},{1,3},{2,0},{3,1},{4,6},{5,7},{6,4},{7,5},{8,10},{9,11},{10,... | collective-permute-start | bytes 13832 | tf_op jit(solution)/shard_map/ppermute | solution.py:138
  8.5 10.0 %collective-permute-start = (bf16[96,768]{1,0:T(8,128)(2,1)S(1)}, bf16[96,768]{1,0:T(8,128)(2,1)}, u32[]{:S(2)}, u32[]{:S(2)}) collective-permute-start(bf16[96,768]{1,0:T(8,128)(2,1)S(1)} %pad_maximum_fusion.34), channel_id=1, source_target_pairs={{0,16},{4,20},{8,24},{12,28},{16,0},{20,4},{24,8},{28,12},{1,17},{... | collective-permute-start | bytes 442376 | tf_op jit(solution)/shard_map/ppermute | solution.py:141
  20.9 8.5 %collective-permute-start.1 = (bf16[2,96,768]{2,1,0:T(8,128)(2,1)}, bf16[2,96,768]{2,1,0:T(8,128)(2,1)}, u32[]{:S(2)}, u32[]{:S(2)}) collective-permute-start(bf16[2,96,768]{2,1,0:T(8,128)(2,1)} %pad_maximum_fusion.33), channel_id=1, source_target_pairs={{0,8},{4,12},{8,0},{12,4},{16,24},{20,28},{24,16},{28,20},{1,9},{5... | collective-permute-start | bytes 884744 | tf_op jit(solution)/shard_map/ppermute | solution.py:141
  30.6 7.4 %collective-permute-start.5 = (bf16[4,96,384]{2,1,0:T(8,128)(2,1)S(1)}, bf16[4,96,384]{2,1,0:T(8,128)(2,1)S(1)}, u32[]{:S(2)}, u32[]{:S(2)}) collective-permute-start(bf16[4,96,384]{2,1,0:T(8,128)(2,1)S(1)} %get-tuple-element.163), channel_id=1, source_target_pairs={{0,2},{1,3},{2,0},{3,1},{4,6},{5,7},{6,4},{7,5},{8,10},{9,11},{10,... | collective-permute-start | bytes 884744 | tf_op jit(solution)/shard_map/ppermute | solution.py:138
  31.2 7.0 %collective-permute-start.2 = (bf16[4,96,384]{2,1,0:T(8,128)(2,1)S(1)}, bf16[4,96,384]{2,1,0:T(8,128)(2,1)S(1)}, u32[]{:S(2)}, u32[]{:S(2)}) collective-permute-start(bf16[4,96,384]{2,1,0:T(8,128)(2,1)S(1)} %get-tuple-element.164), channel_id=1, source_target_pairs={{0,4},{4,0},{8,12},{12,8},{16,20},{20,16},{24,28},{28,24},{1,5},{5... | collective-permute-start | bytes 884744 | tf_op jit(solution)/shard_map/ppermute | solution.py:141
  33.9 14.3 %collective-permute-start.8 = (bf16[96,1536]{1,0:T(8,128)(2,1)S(1)}, bf16[96,1536]{1,0:T(8,128)(2,1)S(1)}, u32[]{:S(2)}, u32[]{:S(2)}) collective-permute-start(bf16[96,1536]{1,0:T(8,128)(2,1)S(1)} %pad_maximum_fusion.32), channel_id=1, source_target_pairs={{0,16},{4,20},{8,24},{12,28},{16,0},{20,4},{24,8},{28,12},{1,17},{... | collective-permute-start | bytes 884744 | tf_op jit(solution)/shard_map/ppermute | solution.py:141
  38.6 12.6 %collective-permute-start.6 = (bf16[2,4,96,384]{3,2,1,0:T(8,128)(2,1)S(1)}, bf16[2,4,96,384]{3,2,1,0:T(8,128)(2,1)S(1)}, u32[]{:S(2)}, u32[]{:S(2)}) collective-permute-start(bf16[2,4,96,384]{3,2,1,0:T(8,128)(2,1)S(1)} %pad_maximum_fusion.23), channel_id=1, source_target_pairs={{0,4},{4,0},{8,12},{12,8},{16,20},{20,16},{24,28},{28,24},{1,5},{5... | collective-permute-start | bytes 1769480 | tf_op jit(solution)/shard_map/ppermute | solution.py:141
  40.1 12.5 %collective-permute-start.3 = (bf16[8,96,384]{2,1,0:T(8,128)(2,1)S(1)}, bf16[8,96,384]{2,1,0:T(8,128)(2,1)S(1)}, u32[]{:S(2)}, u32[]{:S(2)}) collective-permute-start(bf16[8,96,384]{2,1,0:T(8,128)(2,1)S(1)} %bitcast.360), channel_id=1, source_target_pairs={{0,2},{1,3},{2,0},{3,1},{4,6},{5,7},{6,4},{7,5},{8,10},{9,11},{10,... | collective-permute-start | bytes 1769480 | tf_op jit(solution)/shard_map/ppermute | solution.py:138
  49.1 33.4 %collective-permute-start.9 = (bf16[2,96,1536]{2,1,0:T(8,128)(2,1)}, bf16[2,96,1536]{2,1,0:T(8,128)(2,1)}, u32[]{:S(2)}, u32[]{:S(2)}) collective-permute-start(bf16[2,96,1536]{2,1,0:T(8,128)(2,1)} %pad_maximum_fusion.25), channel_id=1, source_target_pairs={{0,8},{4,12},{8,0},{12,4},{16,24},{20,28},{24,16},{28,20},{1,9},{5... | collective-permute-start | bytes 1769480 | tf_op jit(solution)/shard_map/ppermute | solution.py:141
  82.4 4.5 %collective-permute-start.7 = (bf16[320,768]{1,0:T(8,128)(2,1)S(1)}, bf16[320,768]{1,0:T(8,128)(2,1)S(1)}, u32[]{:S(2)}, u32[]{:S(2)}) collective-permute-start(bf16[320,768]{1,0:T(8,128)(2,1)S(1)} %dynamic-slice_convert_fusion.7), channel_id=1, source_target_pairs={{0,1},{1,0},{2,3},{3,2},{4,5},{5,4},{6,7},{7,6},{8,9},{9,8},{10,11... | collective-permute-start | bytes 1474568 | tf_op jit(solution)/shard_map/ppermute | solution.py:135
  83.9 15.8 %collective-permute-start.13 = (bf16[4,96,768]{2,1,0:T(8,128)(2,1)S(1)}, bf16[4,96,768]{2,1,0:T(8,128)(2,1)S(1)}, u32[]{:S(2)}, u32[]{:S(2)}) collective-permute-start(bf16[4,96,768]{2,1,0:T(8,128)(2,1)S(1)} %get-tuple-element.130), channel_id=1, source_target_pairs={{0,2},{1,3},{2,0},{3,1},{4,6},{5,7},{6,4},{7,5},{8,10},{9,11},{10,... | collective-permute-start | bytes 1769480 | tf_op jit(solution)/shard_map/ppermute | solution.py:138
  85.4 15.4 %collective-permute-start.10 = (bf16[4,96,768]{2,1,0:T(8,128)(2,1)S(1)}, bf16[4,96,768]{2,1,0:T(8,128)(2,1)S(1)}, u32[]{:S(2)}, u32[]{:S(2)}) collective-permute-start(bf16[4,96,768]{2,1,0:T(8,128)(2,1)S(1)} %get-tuple-element.131), channel_id=1, source_target_pairs={{0,4},{4,0},{8,12},{12,8},{16,20},{20,16},{24,28},{28,24},{1,5},{5... | collective-permute-start | bytes 1769480 | tf_op jit(solution)/shard_map/ppermute | solution.py:141
  102.2 27.5 %collective-permute-start.14 = (bf16[2,4,96,768]{3,2,1,0:T(8,128)(2,1)}, bf16[2,4,96,768]{3,2,1,0:T(8,128)(2,1)}, u32[]{:S(2)}, u32[]{:S(2)}) collective-permute-start(bf16[2,4,96,768]{3,2,1,0:T(8,128)(2,1)} %pad_maximum_fusion.13), channel_id=1, source_target_pairs={{0,4},{4,0},{8,12},{12,8},{16,20},{20,16},{24,28},{28,24},{1,5},{5... | collective-permute-start | bytes 3538952 | tf_op jit(solution)/shard_map/ppermute | solution.py:141
  104.7 2.2 collective-permute-start.12
  104.9 28.6 %collective-permute-start.11 = (bf16[8,96,768]{2,1,0:T(8,128)(2,1)S(1)}, bf16[8,96,768]{2,1,0:T(8,128)(2,1)}, u32[]{:S(2)}, u32[]{:S(2)}) collective-permute-start(bf16[8,96,768]{2,1,0:T(8,128)(2,1)S(1)} %bitcast.349), channel_id=1, source_target_pairs={{0,2},{1,3},{2,0},{3,1},{4,6},{5,7},{6,4},{7,5},{8,10},{9,11},{10,... | collective-permute-start | bytes 3538952 | tf_op jit(solution)/shard_map/ppermute | solution.py:138
  168.4 6.7 %collective-permute-start.17 = (bf16[320,768]{1,0:T(8,128)(2,1)S(1)}, bf16[320,768]{1,0:T(8,128)(2,1)S(1)}, u32[]{:S(2)}, u32[]{:S(2)}) collective-permute-start(bf16[320,768]{1,0:T(8,128)(2,1)S(1)} %dynamic-slice_convert_fusion.5), channel_id=1, source_target_pairs={{0,1},{1,0},{2,3},{3,2},{4,5},{5,4},{6,7},{7,6},{8,9},{9,8},{10,11... | collective-permute-start | bytes 1474568 | tf_op jit(solution)/shard_map/ppermute | solution.py:135
  173.7 119.1 %collective-permute-start.30 = (bf16[4,2,96,768]{3,2,0,1:T(8,128)(2,1)}, bf16[4,2,96,768]{3,2,0,1:T(8,128)(2,1)}, u32[]{:S(2)}, u32[]{:S(2)}) collective-permute-start(bf16[4,2,96,768]{3,2,0,1:T(8,128)(2,1)} %fusion.44), channel_id=1, source_target_pairs={{0,2},{1,3},{2,0},{3,1},{4,6},{5,7},{6,4},{7,5},{8,10},{9,11},{10,... | collective-permute-start | bytes 3538952 | tf_op jit(solution)/shard_map/ppermute | solution.py:138
  179.5 4.8 %collective-permute-start.18 = (bf16[320,768]{1,0:T(8,128)(2,1)S(1)}, bf16[320,768]{1,0:T(8,128)(2,1)S(1)}, u32[]{:S(2)}, u32[]{:S(2)}) collective-permute-start(bf16[320,768]{1,0:T(8,128)(2,1)S(1)} %get-tuple-element.109), channel_id=1, source_target_pairs={{0,1},{1,0},{2,3},{3,2},{4,5},{5,4},{6,7},{7,6},{8,9},{9,8},{10,11... | collective-permute-start | bytes 1474568 | tf_op jit(solution)/shard_map/ppermute | solution.py:135
  183.8 111.4 %collective-permute-start.28 = (bf16[2,4,96,768]{3,2,1,0:T(8,128)(2,1)}, bf16[2,4,96,768]{3,2,1,0:T(8,128)(2,1)}, u32[]{:S(2)}, u32[]{:S(2)}) collective-permute-start(bf16[2,4,96,768]{3,2,1,0:T(8,128)(2,1)} %fusion.45), channel_id=1, source_target_pairs={{0,4},{4,0},{8,12},{12,8},{16,20},{20,16},{24,28},{28,24},{1,5},{5... | collective-permute-start | bytes 3538952 | tf_op jit(solution)/shard_map/ppermute | solution.py:141
  225.9 73.4 %collective-permute-start.24 = (bf16[4,2,96,384]{3,2,0,1:T(8,128)(2,1)}, bf16[4,2,96,384]{3,2,0,1:T(8,128)(2,1)}, u32[]{:S(2)}, u32[]{:S(2)}) collective-permute-start(bf16[4,2,96,384]{3,2,0,1:T(8,128)(2,1)} %fusion.67), channel_id=1, source_target_pairs={{0,2},{1,3},{2,0},{3,1},{4,6},{5,7},{6,4},{7,5},{8,10},{9,11},{10,... | collective-permute-start | bytes 1769480 | tf_op jit(solution)/shard_map/ppermute | solution.py:138
  289.6 9.3 %collective-permute-start.19 = (bf16[320,768]{1,0:T(8,128)(2,1)S(1)}, bf16[320,768]{1,0:T(8,128)(2,1)S(1)}, u32[]{:S(2)}, u32[]{:S(2)}) collective-permute-start(bf16[320,768]{1,0:T(8,128)(2,1)S(1)} %dynamic-slice_convert_fusion.4), channel_id=1, source_target_pairs={{0,1},{1,0},{2,3},{3,2},{4,5},{5,4},{6,7},{7,6},{8,9},{9,8},{10,11... | collective-permute-start | bytes 1474568 | tf_op jit(solution)/shard_map/ppermute | solution.py:135
  289.8 16.5 %collective-permute-start.22 = (bf16[2,4,96,384]{3,2,1,0:T(8,128)(2,1)S(1)}, bf16[2,4,96,384]{3,2,1,0:T(8,128)(2,1)S(1)}, u32[]{:S(2)}, u32[]{:S(2)}) collective-permute-start(bf16[2,4,96,384]{3,2,1,0:T(8,128)(2,1)S(1)} %fusion.63), channel_id=1, source_target_pairs={{0,4},{4,0},{8,12},{12,8},{16,20},{20,16},{24,28},{28,24},{1,5},{5... | collective-permute-start | bytes 1769480 | tf_op jit(solution)/shard_map/ppermute | solution.py:141
  295.2 23.8 %collective-permute-start.31 = (bf16[4,96,768]{2,1,0:T(8,128)(2,1)S(1)}, bf16[4,96,768]{2,1,0:T(8,128)(2,1)S(1)}, u32[]{:S(2)}, u32[]{:S(2)}) collective-permute-start(bf16[4,96,768]{2,1,0:T(8,128)(2,1)S(1)} %fusion.65), channel_id=1, source_target_pairs={{0,4},{4,0},{8,12},{12,8},{16,20},{20,16},{24,28},{28,24},{1,5},{5... | collective-permute-start | bytes 1769480 | tf_op jit(solution)/shard_map/ppermute | solution.py:141
  297.1 22.0 %collective-permute-start.29 = (bf16[4,96,768]{2,1,0:T(8,128)(2,1)S(1)}, bf16[4,96,768]{2,1,0:T(8,128)(2,1)S(1)}, u32[]{:S(2)}, u32[]{:S(2)}) collective-permute-start(bf16[4,96,768]{2,1,0:T(8,128)(2,1)S(1)} %fusion.64), channel_id=1, source_target_pairs={{0,2},{1,3},{2,0},{3,1},{4,6},{5,7},{6,4},{7,5},{8,10},{9,11},{10,... | collective-permute-start | bytes 1769480 | tf_op jit(solution)/shard_map/ppermute | solution.py:138
  299.1 31.4 %collective-permute-start.20 = (bf16[320,768]{1,0:T(8,128)(2,1)S(1)}, bf16[320,768]{1,0:T(8,128)(2,1)S(1)}, u32[]{:S(2)}, u32[]{:S(2)}) collective-permute-start(bf16[320,768]{1,0:T(8,128)(2,1)S(1)} %add_convert_fusion.1), channel_id=1, source_target_pairs={{0,2},{1,3},{2,0},{3,1},{4,6},{5,7},{6,4},{7,5},{8,10},{9,11},{10,... | collective-permute-start | bytes 1474568 | tf_op jit(solution)/shard_map/ppermute | solution.py:138
  300.7 24.4 %collective-permute-start.25 = (bf16[4,96,384]{2,1,0:T(8,128)(2,1)S(1)}, bf16[4,96,384]{2,1,0:T(8,128)(2,1)S(1)}, u32[]{:S(2)}, u32[]{:S(2)}) collective-permute-start(bf16[4,96,384]{2,1,0:T(8,128)(2,1)S(1)} %fusion.81), channel_id=1, source_target_pairs={{0,4},{4,0},{8,12},{12,8},{16,20},{20,16},{24,28},{28,24},{1,5},{5... | collective-permute-start | bytes 884744 | tf_op jit(solution)/shard_map/ppermute | solution.py:141
  306.5 22.9 %collective-permute-start.23 = (bf16[4,96,384]{2,1,0:T(8,128)(2,1)S(1)}, bf16[4,96,384]{2,1,0:T(8,128)(2,1)S(1)}, u32[]{:S(2)}, u32[]{:S(2)}) collective-permute-start(bf16[4,96,384]{2,1,0:T(8,128)(2,1)S(1)} %fusion.80), channel_id=1, source_target_pairs={{0,2},{1,3},{2,0},{3,1},{4,6},{5,7},{6,4},{7,5},{8,10},{9,11},{10,... | collective-permute-start | bytes 884744 | tf_op jit(solution)/shard_map/ppermute | solution.py:138
  319.6 22.4 %collective-permute-start.32 = (bf16[2,96,1536]{2,1,0:T(8,128)(2,1)S(1)}, bf16[2,96,1536]{2,1,0:T(8,128)(2,1)S(1)}, u32[]{:S(2)}, u32[]{:S(2)}) collective-permute-start(bf16[2,96,1536]{2,1,0:T(8,128)(2,1)S(1)} %fusion.66), channel_id=1, source_target_pairs={{0,8},{4,12},{8,0},{12,4},{16,24},{20,28},{24,16},{28,20},{1,9},{5... | collective-permute-start | bytes 1769480 | tf_op jit(solution)/shard_map/ppermute | solution.py:141
  329.6 11.3 %collective-permute-start.26 = (bf16[2,96,768]{2,1,0:T(8,128)(2,1)S(1)}, bf16[2,96,768]{2,1,0:T(8,128)(2,1)S(1)}, u32[]{:S(2)}, u32[]{:S(2)}) collective-permute-start(bf16[2,96,768]{2,1,0:T(8,128)(2,1)S(1)} %fusion.82), channel_id=1, source_target_pairs={{0,8},{4,12},{8,0},{12,4},{16,24},{20,28},{24,16},{28,20},{1,9},{5... | collective-permute-start | bytes 884744 | tf_op jit(solution)/shard_map/ppermute | solution.py:141
  330.7 33.6 %collective-permute-start.21 = (bf16[2,320,768]{2,1,0:T(8,128)(2,1)S(1)}, bf16[2,320,768]{2,1,0:T(8,128)(2,1)}, u32[]{:S(2)}, u32[]{:S(2)}) collective-permute-start(bf16[2,320,768]{2,1,0:T(8,128)(2,1)S(1)} %pad_maximum_fusion.19), channel_id=1, source_target_pairs={{0,1},{1,0},{2,3},{3,2},{4,5},{5,4},{6,7},{7,6},{8,9},{9,8},{10,11... | collective-permute-start | bytes 2949128 | tf_op jit(solution)/shard_map/ppermute | solution.py:135
  341.0 15.4 %collective-permute-start.27 = (bf16[96,768]{1,0:T(8,128)(2,1)S(1)}, bf16[96,768]{1,0:T(8,128)(2,1)S(1)}, u32[]{:S(2)}, u32[]{:S(2)}) collective-permute-start(bf16[96,768]{1,0:T(8,128)(2,1)S(1)} %fusion.86), channel_id=1, source_target_pairs={{0,16},{4,20},{8,24},{12,28},{16,0},{20,4},{24,8},{28,12},{1,17},{... | collective-permute-start | bytes 442376 | tf_op jit(solution)/shard_map/ppermute | solution.py:141
  342.2 20.3 %collective-permute-start.33 = (bf16[96,1536]{1,0:T(8,128)(2,1)S(1)}, bf16[96,1536]{1,0:T(8,128)(2,1)}, u32[]{:S(2)}, u32[]{:S(2)}) collective-permute-start(bf16[96,1536]{1,0:T(8,128)(2,1)S(1)} %fusion.83), channel_id=1, source_target_pairs={{0,16},{4,20},{8,24},{12,28},{16,0},{20,4},{24,8},{28,12},{1,17},{... | collective-permute-start | bytes 884744 | tf_op jit(solution)/shard_map/ppermute | solution.py:141
  (63 other events, 413.9 us)
